TPU v7x, 32 devices: a whole 2x2x4 slice. The times are simulated.
32 devices in a mesh: term: 8 (over y, x, core), topic: 4 (over z).
Axes of the slice: x: 2, y: 2, z: 4, core: 2. Of those that a mesh axis runs over, the one named last changes fastest.
Arguments:
- factor: bfloat16 [65536, 512], P('term', 'topic'), may hold values from 1e-06 to 0.05, as said below
- tile_values: bfloat16 [65536, 128], P('term'), may hold values from 0.049804688 to 1
- tile_docs: int32 [8, 128], P('term'), may hold values from 0 to 127, as said below
- codes: float32 [512, 128], P('topic', 'term'), may hold values from 0.1 to 2
- gram_stat: float32 [512, 512], P('topic', 'term'), may hold values from 0 to 4
- data_stat: float32 [65536, 512], P('term', 'topic'), may hold values from 0 to 0.4
Outputs:
- codes_out: float32 [512, 128], P('topic', 'term')
- gram_new: float32 [512, 512], P('topic', 'term')
- data_new: float32 [65536, 512], P('term', 'topic')
Inputs may be any that keep to these rules, and one draw needn't show every extreme that they name: `tile_docs`: each row lists 128 different document numbers. `factor`: positive entries.
All inputs are finite; a program needn't handle non-finite values.
Results may differ from a plain program's by a relative error of at most 0.0003.
Values may be sent and summed in bfloat16 or wider, within the bound.
No kernel may reach another device: no remote copies, remote signals or barrier semaphores. Data moves between devices by JAX's collectives and lax.ppermute only.
A program may use at most 128 MiB of HBM per device.

v0:
```python
import jax
import jax.numpy as jnp
from jax import lax
from jax.sharding import PartitionSpec as P

ITERS = 3
EPSILON = 1e-06
DECAY = 0.5


def contract_rows(left, right):
    return lax.dot_general(
        left, right, (((0,), (0,)), ((), ())), preferred_element_type=jnp.float32
    )


def apply_gram(gram_rows, current):
    return jnp.dot(
        gram_rows,
        lax.all_gather(current, "topic", axis=0, tiled=True),
        precision=lax.Precision.HIGHEST,
        preferred_element_type=jnp.float32,
    )


def per_device(factor, tile_values, tile_docs, codes, gram_stat, data_stat):
    term_count = lax.axis_size("term")
    documents = codes.shape[1] * term_count
    onehot = (tile_docs[0][:, None] == jnp.arange(documents, dtype=jnp.int32)[None, :]).astype(
        jnp.bfloat16
    )
    batch = jnp.dot(tile_values, onehot, preferred_element_type=jnp.float32).astype(jnp.bfloat16)
    partial_data = contract_rows(factor, batch)
    data_share = lax.psum_scatter(partial_data, "term", scatter_dimension=1, tiled=True)
    row_block = lax.all_to_all(factor, "topic", split_axis=0, concat_axis=1, tiled=True)
    gram_part = lax.psum_scatter(
        contract_rows(row_block, row_block), "topic", scatter_dimension=0, tiled=True
    )
    gram_rows = lax.psum(gram_part, "term")
    current = codes
    for update in range(ITERS):
        current = current * data_share / (apply_gram(gram_rows, current) + EPSILON)
    outer = lax.dot_general(
        current,
        lax.all_gather(current, "topic", axis=0, tiled=True),
        (((1,), (1,)), ((), ())),
        precision=lax.Precision.HIGHEST,
        preferred_element_type=jnp.float32,
    )
    outer_share = lax.psum_scatter(outer, "term", scatter_dimension=1, tiled=True)
    gram_new = DECAY * gram_stat + outer_share / documents
    code_row = lax.all_gather(current, "term", axis=1, tiled=True)
    widened = batch.astype(jnp.float32)
    product = lax.dot_general(
        widened,
        code_row,
        (((1,), (1,)), ((), ())),
        precision=lax.Precision.HIGHEST,
        preferred_element_type=jnp.float32,
    )
    data_new = DECAY * data_stat + product / documents
    return (current, gram_new, data_new)


def solution(mesh):
    placed = (
        P("term", "topic"),
        P("term", None),
        P("term", None),
        P("topic", "term"),
        P("topic", "term"),
        P("term", "topic"),
    )
    return jax.shard_map(
        per_device,
        mesh=mesh,
        in_specs=placed,
        out_specs=(P("topic", "term"), P("topic", "term"), P("term", "topic")),
        check_vma=False,
    )
```

profile of v0, /device:TPU:0, one launch (start us, length us, event | category | flops | bytes accessed | tf_op | source)
XLA Modules:
  0.0 284.7 jit_solution(639582228280729309)
XLA Ops:
  7.2 54.8 %all_to_all.19 = bf16[4,2048,128]{2,1,0:T(8,128)(2,1)} all-to-all(bf16[4,2048,128]{2,1,0:T(8,128)(2,1)} %bitcast.21), channel_id=1, replica_groups=mesh['term'=8,'topic'=4] {'topic'}, dimensions={0} | all-to-all | bytes 4194304 | tf_op jit(solution)/shard_map/all_to_all | solution.py:35
  62.0 3.9 %copy.9 = bf16[2048,4,128]{0,2,1:T(8,128)(2,1)} copy(bf16[2048,4,128]{2,0,1:T(8,128)(2,1)} %bitcast.22) | data formatting | bytes 4194304 | tf_op jit(solution)/shard_map/all_to_all | solution.py:35
  66.0 4.5 %fusion.7 = f32[512,512]{1,0:T(8,128)} fusion(bf16[2048,512]{0,1:T(8,128)(2,1)} %bitcast.23), kind=kOutput, calls=%fused_computation.14 | convolution fusion | flops 1073741824 | bytes 3145728 | tf_op jit(solution)/shard_map/dot_general | solution.py:12
  70.5 0.0 reduce-scatter.4.cloned.1.call-start
  70.6 0.8 convolution_convert_fusion
  71.4 1.3 copy-done.1
  72.7 1.3 convolution_bitcast_fusion
  74.1 0.0 all-reduce.2.cloned.1.call-start
  74.1 23.0 %reduce-scatter.6.cloned.1.call-done = f32[128,512]{1,0:T(8,128)} async-done(((f32[512,512]{1,0:T(8,128)}), f32[128,512]{1,0:T(8,128)}) %reduce-scatter.6.cloned.1.call-update) | async-done | bytes 262160 | tf_op jit(solution)/shard_map/reduce_scatter | solution.py:36
  97.2 0.0 reduce-scatter.8.cloned.1.call-start
  97.3 13.1 %all_gather.15 = f32[512,16]{0,1:T(8,128)S(1)} all-gather(f32[128,16]{0,1:T(8,128)S(1)} %copy-done.5), channel_id=1, replica_groups=mesh['term'=8,'topic'=4] {'topic'}, dimensions={0}, use_global_device_ids=true | all-gather | bytes 40960 | tf_op jit(solution)/shard_map/all_gather | solution.py:20
  110.4 22.4 %reduce-scatter.4.cloned.1.call-done = f32[128,16]{0,1:T(8,128)} async-done(((f32[128,128]{0,1:T(8,128)}), f32[128,16]{0,1:T(8,128)}) %reduce-scatter.4.cloned.1.call-update) | async-done | bytes 8208 | tf_op jit(solution)/shard_map/reduce_scatter | solution.py:34
  132.8 57.0 %all-reduce.2.cloned.1.call-done = f32[128,512]{1,0:T(8,128)} async-done(((f32[128,512]{1,0:T(8,128)}), f32[128,512]{1,0:T(8,128)}) %all-reduce.2.cloned.1.call-update) | async-done | bytes 262160 | tf_op jit(solution)/shard_map/psum | solution.py:39
  189.8 1.3 fusion.3
  191.0 13.2 %all_gather.16 = f32[512,16]{0,1:T(8,128)S(1)} all-gather(f32[128,16]{0,1:T(8,128)S(1)} %fusion.3), channel_id=1, replica_groups=mesh['term'=8,'topic'=4] {'topic'}, dimensions={0}, use_global_device_ids=true | all-gather | bytes 40960 | tf_op jit(solution)/shard_map/all_gather | solution.py:20
  204.2 1.3 fusion.2
  205.5 13.1 %all_gather.17 = f32[512,16]{0,1:T(8,128)S(1)} all-gather(f32[128,16]{0,1:T(8,128)S(1)} %fusion.2), channel_id=1, replica_groups=mesh['term'=8,'topic'=4] {'topic'}, dimensions={0}, use_global_device_ids=true | all-gather | bytes 40960 | tf_op jit(solution)/shard_map/all_gather | solution.py:20
  218.6 1.3 fusion.1
  219.9 8.6 %all_gather.19 = f32[128,128]{0,1:T(8,128)S(1)} all-gather(f32[128,16]{0,1:T(8,128)S(1)} %fusion.1), channel_id=1, replica_groups=mesh['term'=8,'topic'=4] {'term'}, dimensions={1}, use_global_device_ids=true | all-gather | bytes 73728 | tf_op jit(solution)/shard_map/all_gather | solution.py:52
  228.6 13.1 %all_gather.18 = f32[512,16]{0,1:T(8,128)S(1)} all-gather(f32[128,16]{0,1:T(8,128)S(1)} %fusion.1), channel_id=1, replica_groups=mesh['term'=8,'topic'=4] {'topic'}, dimensions={0}, use_global_device_ids=true | all-gather | bytes 40960 | tf_op jit(solution)/shard_map/all_gather | solution.py:45
  241.7 1.3 fusion.8
  243.0 7.4 %fusion = f32[8192,128]{1,0:T(8,128)} fusion(bf16[128,8192]{1,0:T(8,128)(2,1)} %copy-done.1, f32[128,128]{0,1:T(8,128)S(1)} %all_gather.19, f32[8192,128]{1,0:T(8,128)} %param.11), kind=kOutput, calls=%fused_computation.1 | convolution fusion | flops 1613758464 | bytes 10551296 | tf_op jit(solution)/shard_map/dot_general | solution.py:54
  250.4 26.5 %reduce-scatter.8.cloned.1.call-done = f32[128,64]{0,1:T(8,128)} async-done(((f32[128,512]{0,1:T(8,128)}), f32[128,64]{0,1:T(8,128)}) %reduce-scatter.8.cloned.1.call-update) | async-done | bytes 32784 | tf_op jit(solution)/shard_map/reduce_scatter | solution.py:50
  276.8 1.4 multiply_add_fusion
  (18 shorter events, 0.1 us)
Async XLA Ops:
  7.2 63.4 %copy-start = (bf16[8192,128]{1,0:T(8,128)(2,1)S(1)}, bf16[8192,128]{1,0:T(8,128)(2,1)}, u32[]{:S(2)}) copy-start(bf16[8192,128]{1,0:T(8,128)(2,1)} %param.7) | copy-start | bytes 6291460
  7.2 90.0 %reduce-scatter.6.cloned.1.call-start = ((), (), s32[]{:S(2)}) async-start(), calls=%async_computation.5 | async-start | bytes 1310720 | tf_op jit(solution)/shard_map/reduce_scatter | solution.py:36
  66.0 4.6 %copy-start.6 = (s32[1,128]{1,0:T(1,128)S(1)}, s32[1,128]{1,0:T(1,128)}, u32[]{:S(2)}) copy-start(s32[1,128]{1,0:T(1,128)} %param.8) | copy-start | bytes 1540
  70.5 62.3 %reduce-scatter.4.cloned.1.call-start = ((), (), s32[]{:S(2)}) async-start(), calls=%async_computation.4 | async-start | bytes 73728 | tf_op jit(solution)/shard_map/reduce_scatter | solution.py:34
  70.6 2.2 copy-start.2
  71.4 1.3 copy-start.1
  72.7 24.5 %copy-start.5 = (f32[128,16]{0,1:T(8,128)S(1)}, f32[128,16]{0,1:T(8,128)}, u32[]{:S(2)}) copy-start(f32[128,16]{0,1:T(8,128)} %param.9) | copy-start | bytes 24580
  74.1 115.7 %all-reduce.2.cloned.1.call-start = ((), (), s32[]{:S(2)}) async-start(), calls=%async_computation.6 | async-start | bytes 524288 | tf_op jit(solution)/shard_map/psum | solution.py:39
  97.2 179.6 %reduce-scatter.8.cloned.1.call-start = ((), (), s32[]{:S(2)}) async-start(), calls=%async_computation.7 | async-start | bytes 294912 | tf_op jit(solution)/shard_map/reduce_scatter | solution.py:50
  219.9 30.4 %copy-start.3 = (f32[128,16]{0,1:T(8,128)}, f32[128,16]{0,1:T(8,128)S(1)}, u32[]{:S(2)}) copy-start(f32[128,16]{0,1:T(8,128)S(1)} %fusion.1) | copy-start | bytes 24580
  243.0 33.8 %copy-start.4 = (f32[128,64]{0,1:T(8,128)S(1)}, f32[128,64]{0,1:T(8,128)}, u32[]{:S(2)}) copy-start(f32[128,64]{0,1:T(8,128)} %param.10) | copy-start | bytes 98308
Sparse Core Ops, SparseCore 0:
  70.6 26.5 reduce-scatter.5
  100.7 31.9 reduce-scatter.3
  135.8 53.8 all-reduce.1
  243.1 33.6 reduce-scatter.7
where the time goes:
time: 285 us
  waiting for transfers between devices  129 us (45%)
  blocking collectives  116 us (41%)
  matrix products  19.1 us (7%)
  between operations  13.9 us (5%)
  local copies, waits for them, and re-layouts  5.32 us (2%)
    psum x1, waiting for transfers between devices, per_device(): gram_rows = lax.psum(gram_part, 'term')  57 us
    all_to_all x1, blocking collectives, per_device(): lax.all_to_all(factor, 'topic', split_axis=0, concat_axis=1, tiled=True)  54.8 us
    all_gather x3, blocking collectives, apply_gram(): lax.all_gather(current, 'topic', axis=0, tiled=True)  39.5 us
    reduce_scatter x1, waiting for transfers between devices, per_device(): lax.psum_scatter(outer, 'term', scatter_dimension=1, tiled=True)  26.5 us
    reduce_scatter x1, waiting for transfers between devices, per_device(): lax.psum_scatter(contract_rows(row_block, row_block), 'topic', scatter_di...  23 us
    reduce_scatter x1, waiting for transfers between devices, per_device(): lax.psum_scatter(partial_data, 'term', scatter_dimension=1, tiled=True)  22.4 us
    all_gather x1, blocking collectives, per_device(): lax.all_gather(current, 'topic', axis=0, tiled=True)  13.1 us
    all_gather x1, blocking collectives, per_device(): code_row = lax.all_gather(current, 'term', axis=1, tiled=True)  8.61 us
  transfers between devices with their start and end apart: 4, of which 4 were waited for; matrix products, arithmetic and copies ran while one was open for 3% of the time, Pallas kernels for 0%

commit v1 on v0

--- a/solution.py
+++ b/solution.py
@@ -36,7 +36,11 @@
     gram_part = lax.psum_scatter(
         contract_rows(row_block, row_block), "topic", scatter_dimension=0, tiled=True
     )
-    gram_rows = lax.psum(gram_part, "term")
+    gram_rows = gram_part
+    for hop in (1, 2, 4):
+        gram_rows = gram_rows + lax.ppermute(
+            gram_rows, "term", [(dev, dev ^ hop) for dev in range(8)]
+        )
     current = codes
     for update in range(ITERS):
         current = current * data_share / (apply_gram(gram_rows, current) + EPSILON)

time: 285 us -> 240 us (0.84)
  waiting for transfers between devices: 129 us -> 78.9 us
  starting transfers between devices: 0.16 us -> 3.18 us
    psum x1 -> x0, waiting for transfers between devices: 57 us -> none  [per_device(): gram_rows = lax.psum(gram_part, 'term')]
    ppermute x0 -> x3, waiting for transfers between devices: none -> 7.79 us  [per_device(): lax.ppermute(gram_rows, 'term', [(dev, dev ^ hop) for dev in range(8)])]
    reduce_scatter x1, waiting for transfers between devices: 22.4 us -> 18 us  [per_device(): lax.psum_scatter(partial_data, 'term', scatter_dimension=1, tiled=True)]
    reduce_scatter x1, waiting for transfers between devices: 23 us -> 26.6 us  [per_device(): lax.psum_scatter(contract_rows(row_block, row_block), 'topic', scatter_di...]
    ppermute x0 -> x3, starting transfers between devices: none -> 3.06 us  [per_device(): lax.ppermute(gram_rows, 'term', [(dev, dev ^ hop) for dev in range(8)])]
  transfers between devices with their start and end apart: 4 -> 6, of which waited for: 4 -> 5; matrix products, arithmetic and copies ran while one was open for 3% -> 4% of each run, Pallas kernels for 0% -> 0%
where the time goes in v1:
time: 240 us; the launch traced here: 239 us
  blocking collectives  117 us (49%)
  waiting for transfers between devices  78.9 us (33%)
  matrix products  18.4 us (8%)
  between operations  15.6 us (6%)
  local copies, waits for them, and re-layouts  3.98 us (2%)
  starting transfers between devices  3.18 us (1%)
  other arithmetic  2.44 us (1%)
    all_to_all x1, blocking collectives, per_device(): lax.all_to_all(factor, 'topic', split_axis=0, concat_axis=1, tiled=True)  54.8 us
    all_gather x3, blocking collectives, apply_gram(): lax.all_gather(current, 'topic', axis=0, tiled=True)  39.5 us
    reduce_scatter x1, waiting for transfers between devices, per_device(): lax.psum_scatter(contract_rows(row_block, row_block), 'topic', scatter_di...  26.6 us
    reduce_scatter x1, waiting for transfers between devices, per_device(): lax.psum_scatter(outer, 'term', scatter_dimension=1, tiled=True)  26.4 us
    reduce_scatter x1, waiting for transfers between devices, per_device(): lax.psum_scatter(partial_data, 'term', scatter_dimension=1, tiled=True)  18 us
    all_gather x1, blocking collectives, per_device(): lax.all_gather(current, 'topic', axis=0, tiled=True)  13.1 us
    all_gather x1, blocking collectives, per_device(): code_row = lax.all_gather(current, 'term', axis=1, tiled=True)  9.2 us
    ppermute x3, waiting for transfers between devices, per_device(): lax.ppermute(gram_rows, 'term', [(dev, dev ^ hop) for dev in range(8)])  7.79 us
  transfers between devices with their start and end apart: 6, of which 5 were waited for; matrix products, arithmetic and copies ran while one was open for 4% of the time, Pallas kernels for 0%

profile of v1, /device:TPU:0, one launch (start us, length us, event | category | flops | bytes accessed | tf_op | source)
XLA Modules:
  0.0 239.0 jit_solution(4860731499453757168)
XLA Ops:
  8.1 54.8 %all_to_all.19 = bf16[4,2048,128]{2,1,0:T(8,128)(2,1)} all-to-all(bf16[4,2048,128]{2,1,0:T(8,128)(2,1)} %bitcast.21), channel_id=1, replica_groups=mesh['term'=8,'topic'=4] {'topic'}, dimensions={0} | all-to-all | bytes 4194304 | tf_op jit(solution)/shard_map/all_to_all | solution.py:35
  62.8 3.9 %copy.9 = bf16[2048,4,128]{0,2,1:T(8,128)(2,1)} copy(bf16[2048,4,128]{2,0,1:T(8,128)(2,1)} %bitcast.22) | data formatting | bytes 4194304 | tf_op jit(solution)/shard_map/all_to_all | solution.py:35
  66.8 4.5 %fusion.7 = f32[512,512]{1,0:T(8,128)} fusion(bf16[2048,512]{0,1:T(8,128)(2,1)} %bitcast.23), kind=kOutput, calls=%fused_computation.14 | convolution fusion | flops 1073741824 | bytes 3145728 | tf_op jit(solution)/shard_map/dot_general | solution.py:12
  71.4 26.6 %reduce-scatter.6.cloned.1.call-done = f32[128,512]{1,0:T(8,128)} async-done(((f32[512,512]{1,0:T(8,128)}), f32[128,512]{1,0:T(8,128)}) %reduce-scatter.6.cloned.1.call-update) | async-done | bytes 262160 | tf_op jit(solution)/shard_map/reduce_scatter | solution.py:36
  98.0 1.7 collective-permute-done
  99.7 1.0 add.30
  100.7 1.5 collective-permute-start.1
  102.3 0.8 convolution_convert_fusion
  103.1 6.0 %collective-permute-done.1 = f32[128,512]{1,0:T(8,128)S(1)} collective-permute-done((f32[128,512]{1,0:T(8,128)S(1)}, f32[128,512]{1,0:T(8,128)S(1)}, u32[]{:S(2)}, u32[]{:S(2)}) %collective-permute-start.1) | collective-permute-done | bytes 262176 | tf_op jit(solution)/shard_map/ppermute | solution.py:41
  109.2 1.5 collective-permute-start.2
  110.7 1.3 convolution_bitcast_fusion
  112.1 13.1 %all_gather.15 = f32[512,16]{0,1:T(8,128)S(1)} all-gather(f32[128,16]{0,1:T(8,128)S(1)} %copy-done.5), channel_id=1, replica_groups=mesh['term'=8,'topic'=4] {'topic'}, dimensions={0}, use_global_device_ids=true | all-gather | bytes 40960 | tf_op jit(solution)/shard_map/all_gather | solution.py:20
  125.3 18.0 %reduce-scatter.4.cloned.1.call-done = f32[128,16]{0,1:T(8,128)} async-done(((f32[128,128]{0,1:T(8,128)}), f32[128,16]{0,1:T(8,128)}) %reduce-scatter.4.cloned.1.call-update) | async-done | bytes 8208 | tf_op jit(solution)/shard_map/reduce_scatter | solution.py:34
  143.3 1.0 fusion.3
  144.3 13.2 %all_gather.16 = f32[512,16]{0,1:T(8,128)S(1)} all-gather(f32[128,16]{0,1:T(8,128)S(1)} %fusion.3), channel_id=1, replica_groups=mesh['term'=8,'topic'=4] {'topic'}, dimensions={0}, use_global_device_ids=true | all-gather | bytes 40960 | tf_op jit(solution)/shard_map/all_gather | solution.py:20
  157.5 1.0 fusion.2
  158.6 13.1 %all_gather.17 = f32[512,16]{0,1:T(8,128)S(1)} all-gather(f32[128,16]{0,1:T(8,128)S(1)} %fusion.2), channel_id=1, replica_groups=mesh['term'=8,'topic'=4] {'topic'}, dimensions={0}, use_global_device_ids=true | all-gather | bytes 40960 | tf_op jit(solution)/shard_map/all_gather | solution.py:20
  171.7 1.0 fusion.1
  172.7 9.2 %all_gather.19 = f32[128,128]{0,1:T(8,128)S(1)} all-gather(f32[128,16]{0,1:T(8,128)S(1)} %fusion.1), channel_id=1, replica_groups=mesh['term'=8,'topic'=4] {'term'}, dimensions={1}, use_global_device_ids=true | all-gather | bytes 73728 | tf_op jit(solution)/shard_map/all_gather | solution.py:56
  181.9 13.1 %all_gather.18 = f32[512,16]{0,1:T(8,128)S(1)} all-gather(f32[128,16]{0,1:T(8,128)S(1)} %fusion.1), channel_id=1, replica_groups=mesh['term'=8,'topic'=4] {'topic'}, dimensions={0}, use_global_device_ids=true | all-gather | bytes 40960 | tf_op jit(solution)/shard_map/all_gather | solution.py:49
  195.1 1.3 fusion.8
  196.4 7.4 %fusion = f32[8192,128]{1,0:T(8,128)} fusion(bf16[128,8192]{1,0:T(8,128)(2,1)} %copy-done.1, f32[128,128]{0,1:T(8,128)S(1)} %all_gather.19, f32[8192,128]{1,0:T(8,128)} %param.11), kind=kOutput, calls=%fused_computation.1 | convolution fusion | flops 1613758464 | bytes 10551296 | tf_op jit(solution)/shard_map/dot_general | solution.py:58
  203.8 26.4 %reduce-scatter.8.cloned.1.call-done = f32[128,64]{0,1:T(8,128)} async-done(((f32[128,512]{0,1:T(8,128)}), f32[128,64]{0,1:T(8,128)}) %reduce-scatter.8.cloned.1.call-update) | async-done | bytes 32784 | tf_op jit(solution)/shard_map/reduce_scatter | solution.py:54
  230.2 1.4 multiply_add_fusion
  (24 shorter events, 0.3 us)
Async XLA Ops:
  8.0 94.3 %copy-start = (bf16[8192,128]{1,0:T(8,128)(2,1)S(1)}, bf16[8192,128]{1,0:T(8,128)(2,1)}, u32[]{:S(2)}) copy-start(bf16[8192,128]{1,0:T(8,128)(2,1)} %param.7) | copy-start | bytes 6291460
  8.0 90.0 %reduce-scatter.6.cloned.1.call-start = ((), (), s32[]{:S(2)}) async-start(), calls=%async_computation.5 | async-start | bytes 1310720 | tf_op jit(solution)/shard_map/reduce_scatter | solution.py:36
  66.8 35.5 %copy-start.6 = (s32[1,128]{1,0:T(1,128)S(1)}, s32[1,128]{1,0:T(1,128)}, u32[]{:S(2)}) copy-start(s32[1,128]{1,0:T(1,128)} %param.8) | copy-start | bytes 1540
  71.3 72.0 %reduce-scatter.4.cloned.1.call-start = ((), (), s32[]{:S(2)}) async-start(), calls=%async_computation.4 | async-start | bytes 73728 | tf_op jit(solution)/shard_map/reduce_scatter | solution.py:34
  98.0 1.7 collective-permute-start
  100.7 8.4 %collective-permute-start.1 = (f32[128,512]{1,0:T(8,128)S(1)}, f32[128,512]{1,0:T(8,128)S(1)}, u32[]{:S(2)}, u32[]{:S(2)}) collective-permute-start(f32[128,512]{1,0:T(8,128)S(1)} %add.30), channel_id=1, source_target_pairs={{0,8},{4,12},{8,0},{12,4},{16,24},{20,28},{24,16},{28,20},{1,9},{5... | collective-permute-start | bytes 786440 | tf_op jit(solution)/shard_map/ppermute | solution.py:41
  102.3 8.5 %copy-start.2 = (bf16[8192,128]{1,0:T(8,128)(2,1)S(1)}, bf16[8192,128]{1,0:T(8,128)(2,1)}, u32[]{:S(2)}) copy-start(bf16[8192,128]{1,0:T(8,128)(2,1)} %param.6) | copy-start | bytes 6291460
  103.1 7.6 %copy-start.1 = (bf16[128,8192]{1,0:T(8,128)(2,1)}, bf16[128,8192]{1,0:T(8,128)(2,1)S(1)}, u32[]{:S(2)}) copy-start(bf16[128,8192]{1,0:T(8,128)(2,1)S(1)} %convolution_convert_fusion) | copy-start | bytes 6291460
  109.2 3.0 %copy-start.5 = (f32[128,16]{0,1:T(8,128)S(1)}, f32[128,16]{0,1:T(8,128)}, u32[]{:S(2)}) copy-start(f32[128,16]{0,1:T(8,128)} %param.9) | copy-start | bytes 24580
  109.2 16.1 %collective-permute-start.2 = (f32[128,512]{1,0:T(8,128)S(1)}, f32[128,512]{1,0:T(8,128)S(1)}, u32[]{:S(2)}, u32[]{:S(2)}) collective-permute-start(f32[128,512]{1,0:T(8,128)S(1)} %add.31), channel_id=1, source_target_pairs={{0,16},{4,20},{8,24},{12,28},{16,0},{20,4},{24,8},{28,12},{1,17},{... | collective-permute-start | bytes 786440 | tf_op jit(solution)/shard_map/ppermute | solution.py:41
  112.1 118.1 %reduce-scatter.8.cloned.1.call-start = ((), (), s32[]{:S(2)}) async-start(), calls=%async_computation.6 | async-start | bytes 294912 | tf_op jit(solution)/shard_map/reduce_scatter | solution.py:54
  172.7 31.0 %copy-start.3 = (f32[128,16]{0,1:T(8,128)}, f32[128,16]{0,1:T(8,128)S(1)}, u32[]{:S(2)}) copy-start(f32[128,16]{0,1:T(8,128)S(1)} %fusion.1) | copy-start | bytes 24580
  196.4 33.8 %copy-start.4 = (f32[128,64]{0,1:T(8,128)S(1)}, f32[128,64]{0,1:T(8,128)}, u32[]{:S(2)}) copy-start(f32[128,64]{0,1:T(8,128)} %param.10) | copy-start | bytes 98308
Sparse Core Ops, SparseCore 0:
  71.4 26.5 reduce-scatter.5
Sparse Core Ops, SparseCore 1:
  112.2 31.1 reduce-scatter.3
  196.5 33.7 reduce-scatter.7
